TPU v7x, 512 devices: a whole 4x4x16 slice. The times are simulated.
512 devices in a mesh: clus: 64 (over x, z_hi, y), samp: 8 (over z_lo, core).
Axes of the slice: x: 4, y: 4, z: 16 (z_hi: 4, z_lo: 4; z = z_hi * 4 + z_lo), core: 2. Of those that a mesh axis runs over, the one named last changes fastest.
Arguments:
- child_patterns: float32 [2048, 2, 24, 512], P('clus', None, 'samp'), may hold values from -6 to 6
- theta_weights: float32 [6, 9], replicated, may hold values from -0.4 to 0.6
- phi_stencil: int32 [1024, 6], replicated, may hold values from 0 to 511, as said below
- phi_weights: float32 [1024, 6], replicated, may hold values from -0.3 to 0.7
- shift_phase: float32 [8, 48, 1024], P(None, 'samp'), may hold values from -3.140625 to 3.140625
- translation_table: float32 [16, 2, 48, 1024], P(None, None, 'samp', 'clus'), may hold values from -1.25 to 1.25
- far_list: int32 [256, 12], replicated, may hold values from 0 to 255, as said below
- far_vector: int32 [256, 12], replicated, may hold values from 0 to 15
Outputs:
- parent_incoming: float32 [256, 2, 48, 1024], P('clus', None, 'samp')
- child_incoming: float32 [2048, 2, 24, 512], P('clus', None, 'samp')
Inputs may be any that keep to these rules, and one draw needn't show every extreme that they name: `far_list`: row i names 12 different parent clusters, never i itself. `phi_stencil`: row n names 6 cyclically consecutive child columns starting at n // 2 - 6 // 2 + 1 or one column later.
All inputs are finite; a program needn't handle non-finite values.
Results may differ from a plain program's by a relative error of at most 0.00007.
Values sent between devices are 32-bit elements; how exact they have to be, the bound alone decides.
A program may use at most 128 MiB of HBM per device.

v0:
```python
import jax
import jax.numpy as jnp
from jax import lax
from jax.sharding import PartitionSpec as P

P_SIZE = 6
HIGH = lax.Precision.HIGH


def shifted(value, axis, by):
    peers = lax.axis_size(axis)
    return lax.ppermute(value, axis, [(i, (i + by) % peers) for i in range(peers)])


def phi_table(phi_stencil, phi_weights, columns):
    positions = jnp.arange(columns, dtype=jnp.int32)
    total = jnp.zeros((columns, phi_stencil.shape[0]), jnp.float32)
    for point in range(phi_stencil.shape[1]):
        hits = (phi_stencil[None, :, point] == positions[:, None]).astype(jnp.float32)
        total = total + hits * phi_weights[None, :, point]
    return total


def per_device(
    child_patterns,
    theta_weights,
    phi_stencil,
    phi_weights,
    shift_phase,
    translation_table,
    far_list,
    far_vector,
):
    groups = child_patterns.shape[0] // 8
    columns = child_patterns.shape[3]
    rows_parent = theta_weights.shape[0]
    azimuth = phi_stencil.shape[0]
    margin = P_SIZE // 2
    below = shifted(child_patterns, "samp", 1)
    above = shifted(child_patterns, "samp", -1)
    phi_matrix = phi_table(phi_stencil, phi_weights, columns)
    cosine = jnp.cos(shift_phase)
    sine = jnp.sin(shift_phase)
    extended = jnp.concatenate([below, child_patterns, above], axis=2)
    tilted = jnp.stack(
        [
            sum((theta_weights[a, b] * extended[:, :, b] for b in range(9)))
            for a in range(rows_parent)
        ],
        axis=2,
    )
    refined = jnp.einsum("cqap,pn->cqan", tilted, phi_matrix, precision=HIGH)
    refined = refined.reshape(groups, 8, 2, rows_parent, azimuth)
    real_part = refined[:, :, 0] * cosine - refined[:, :, 1] * sine
    imag_part = refined[:, :, 0] * sine + refined[:, :, 1] * cosine
    outgoing = jnp.stack([jnp.sum(real_part, axis=1), jnp.sum(imag_part, axis=1)], axis=1)
    everyone = lax.all_to_all(outgoing, "clus", split_axis=3, concat_axis=0, tiled=True)
    clusters = everyone.shape[0]
    lanes = everyone.shape[2] * everyone.shape[3]
    flat = everyone.reshape(clusters, 2 * lanes)
    table = translation_table.reshape(translation_table.shape[0], 2 * lanes)
    pick = (far_list[:, :, None] == jnp.arange(clusters)[None, None, :]).astype(jnp.float32)
    pick_vec = (far_vector[:, :, None] == jnp.arange(table.shape[0])[None, None, :]).astype(
        jnp.float32
    )
    source = jnp.einsum("ilc,cs->lis", pick, flat, precision=HIGH)
    operator = jnp.einsum("ilv,vs->lis", pick_vec, table, precision=HIGH)
    s_re, s_im = (source[..., :lanes], source[..., lanes:])
    o_re, o_im = (operator[..., :lanes], operator[..., lanes:])
    in_re = jnp.sum(o_re * s_re - o_im * s_im, axis=0)
    in_im = jnp.sum(o_re * s_im + o_im * s_re, axis=0)
    landed = jnp.concatenate([in_re, in_im], axis=1).reshape(everyone.shape)
    incoming = lax.all_to_all(landed, "clus", split_axis=0, concat_axis=3, tiled=True)
    low_real = incoming[:, None, 0] * cosine + incoming[:, None, 1] * sine
    low_imag = incoming[:, None, 1] * cosine - incoming[:, None, 0] * sine
    lowered = jnp.stack([low_real, low_imag], axis=2).reshape(groups * 8, 2, rows_parent, azimuth)
    narrow = jnp.einsum("cqan,pn->cqap", lowered, phi_matrix, precision=HIGH)

    def back(first):
        return jnp.stack(
            [
                sum((theta_weights[a, b] * narrow[:, :, a] for a in range(rows_parent)))
                for b in range(first, first + margin)
            ],
            axis=2,
        )

    from_above = shifted(back(0), "samp", -1)
    from_below = shifted(back(2 * margin), "samp", 1)
    child_incoming = back(margin) + from_above + from_below
    return (incoming, child_incoming)


def solution(mesh):
    placed = (
        P("clus", None, "samp", None),
        P(),
        P(),
        P(),
        P(None, "samp", None),
        P(None, None, "samp", "clus"),
        P(),
        P(),
    )
    return jax.shard_map(
        per_device,
        mesh=mesh,
        in_specs=placed,
        out_specs=(P("clus", None, "samp", None), P("clus", None, "samp", None)),
        check_vma=False,
    )
```

profile of v0, /device:TPU:1, one launch (start us, length us, event | category | flops | bytes accessed | tf_op | source)
XLA Modules:
  0.0 206.6 jit_solution(3628376807708791519)
XLA Ops:
  0.6 1.1 copy.62
  1.7 4.9 %collective-permute-start = (f32[32,2,3,512]{3,0,2,1:T(8,128)S(1)}, f32[32,2,3,512]{3,0,2,1:T(8,128)S(1)}, u32[]{:S(2)}, u32[]{:S(2)}) collective-permute-start(f32[32,2,3,512]{3,0,2,1:T(8,128)S(1)} %copy.62), channel_id=1, source_target_pairs={{0,1},{1,2},{2,3},{3,4},{4,5},{5,6},{6,7},{7,0},{8,9},{9,10},{10,1... | collective-permute-start | bytes 1179656 | tf_op jit(solution)/shard_map/ppermute | solution.py:12
  6.6 5.7 %collective-permute-start.1 = (f32[32,2,3,512]{3,0,2,1:T(8,128)S(1)}, f32[32,2,3,512]{3,0,2,1:T(8,128)S(1)}, u32[]{:S(2)}, u32[]{:S(2)}) collective-permute-start(f32[32,2,3,512]{3,0,2,1:T(8,128)S(1)} %copy.62), channel_id=1, source_target_pairs={{0,7},{1,0},{2,1},{3,2},{4,3},{5,4},{6,5},{7,6},{8,15},{9,8},{10,9... | collective-permute-start | bytes 1179656 | tf_op jit(solution)/shard_map/ppermute | solution.py:12
  12.4 2.1 %fusion.24 = (f32[1,1]{1,0:T(1,128)}, f32[1,1]{1,0:T(1,128)}, f32[1,1]{1,0:T(1,128)}, f32[1,1]{1,0:T(1,128)}, f32[1,1]{1,0:T(1,128)}, /*index=5*/f32[1,1]{1,0:T(...) fusion(f32[6,9]{1,0:T(8,128)} %param.9), kind=kLoop, calls=%fused_computation.62 | loop fusion | bytes 152 | tf_op jit(solution)/shard_map/slice | solution.py:47
  14.5 1.0 fusion.21
  15.5 1.0 fusion.22
  16.5 2.0 fusion.25
  18.5 2.1 %fusion.23 = (f32[1,1]{1,0:T(1,128)}, f32[1,1]{1,0:T(1,128)}, f32[1,1]{1,0:T(1,128)}, f32[1,1]{1,0:T(1,128)}, f32[1,1]{1,0:T(1,128)}, /*index=5*/f32[1,1]{1,0:T(...) fusion(f32[6,9]{1,0:T(8,128)} %param.9), kind=kLoop, calls=%fused_computation.61 | loop fusion | bytes 152 | tf_op jit(solution)/shard_map/slice | solution.py:47
  20.6 1.6 fusion.20
  22.2 0.0 collective-permute-done
  22.2 0.0 collective-permute-done.1
  22.3 5.6 %add_dynamic-update-slice_fusion.5 = f32[32,2,6,512]{3,0,2,1:T(8,128)S(1)} fusion(f32[32,2,3,512]{3,0,2,1:T(8,128)S(1)} %collective-permute-done.1, f32[32,2,3,512]{3,0,2,1:T(8,128)S(1)} %copy.62, f32[32,2,3,512]{3,0,2,1:T(8,128)S(1)} %collective-permute-done, f32[]{:T(128)} %bitcast.9, f32[]{:T(128)} %bitcast.8, f32[]{:T(128)} %bitcast.7, f32[]{:T(128)} %bitcast.6, ...), kind=kLoop, calls=%fused_computation.50 | loop fusion | flops 557055 | bytes 1310756
  27.8 5.8 %add_dynamic-update-slice_fusion.4 = f32[32,2,6,512]{3,0,2,1:T(8,128)S(1)} fusion(f32[32,2,6,512]{3,0,2,1:T(8,128)S(1)} %add_dynamic-update-slice_fusion.5, f32[32,2,3,512]{3,0,2,1:T(8,128)S(1)} %collective-permute-done.1, f32[32,2,3,512]{3,0,2,1:T(8,128)S(1)} %copy.62, f32[32,2,3,512]{3,0,2,1:T(8,128)S(1)} %collective-permute-done, f32[]{:T(128)} %bitcast.18, ...), kind=kLoop, calls=%fused_computation.49 | loop fusion | flops 557056 | bytes 1310756
  33.7 6.0 %add_dynamic-update-slice_fusion.3 = f32[32,2,6,512]{3,0,2,1:T(8,128)S(1)} fusion(f32[32,2,6,512]{3,0,2,1:T(8,128)S(1)} %add_dynamic-update-slice_fusion.4, f32[32,2,3,512]{3,0,2,1:T(8,128)S(1)} %collective-permute-done.1, f32[32,2,3,512]{3,0,2,1:T(8,128)S(1)} %copy.62, f32[32,2,3,512]{3,0,2,1:T(8,128)S(1)} %collective-permute-done, f32[]{:T(128)} %bitcast.27, ...), kind=kLoop, calls=%fused_computation.48 | loop fusion | flops 557056 | bytes 1310756
  39.7 5.6 %add_dynamic-update-slice_fusion.2 = f32[32,2,6,512]{3,0,2,1:T(8,128)S(1)} fusion(f32[32,2,6,512]{3,0,2,1:T(8,128)S(1)} %add_dynamic-update-slice_fusion.3, f32[32,2,3,512]{3,0,2,1:T(8,128)S(1)} %collective-permute-done.1, f32[32,2,3,512]{3,0,2,1:T(8,128)S(1)} %copy.62, f32[32,2,3,512]{3,0,2,1:T(8,128)S(1)} %collective-permute-done, f32[]{:T(128)} %bitcast.36, ...), kind=kLoop, calls=%fused_computation.47 | loop fusion | flops 557056 | bytes 1310756
  45.3 5.8 %add_dynamic-update-slice_fusion.1 = f32[32,2,6,512]{3,0,2,1:T(8,128)S(1)} fusion(f32[32,2,6,512]{3,0,2,1:T(8,128)S(1)} %add_dynamic-update-slice_fusion.2, f32[32,2,3,512]{3,0,2,1:T(8,128)S(1)} %collective-permute-done.1, f32[32,2,3,512]{3,0,2,1:T(8,128)S(1)} %copy.62, f32[32,2,3,512]{3,0,2,1:T(8,128)S(1)} %collective-permute-done, f32[]{:T(128)} %bitcast.45, ...), kind=kLoop, calls=%fused_computation.46 | loop fusion | flops 557056 | bytes 1310756
  51.1 5.7 %add_dynamic-update-slice_fusion = f32[32,2,6,512]{3,0,2,1:T(8,128)S(1)} fusion(f32[32,2,6,512]{3,0,2,1:T(8,128)S(1)} %add_dynamic-update-slice_fusion.1, f32[32,2,3,512]{3,0,2,1:T(8,128)S(1)} %collective-permute-done.1, f32[32,2,3,512]{3,0,2,1:T(8,128)S(1)} %copy.62, f32[32,2,3,512]{3,0,2,1:T(8,128)S(1)} %collective-permute-done, f32[]{:T(128)} %bitcast.54, ...), kind=kLoop, calls=%fused_computation.45 | loop fusion | flops 557056 | bytes 1310756 | tf_op jit(solution)/shard_map/stack | solution.py:45
  56.8 2.8 %fusion.10 = f32[4,8,2,6,1024]{4,1,0,3,2:T(8,128)S(1)} fusion(f32[32,2,6,512]{3,0,2,1:T(8,128)S(1)} %add_dynamic-update-slice_fusion, f32[1024]{0:T(1024)S(1)} %bitcast.152, s32[1024]{0:T(1024)S(1)} %bitcast.140, f32[1024]{0:T(1024)S(1)} %bitcast.154, s32[1024]{0:T(1024)S(1)} %bitcast.142, f32[1024]{0:T(1024)S(1)} %bitcast.146, s32[1024]{0:T(1024)S(1)} %bitcast.134, ...), kind=kOutput, calls=%fused_computation.19 | convolution fusion | flops 1216872448 | bytes 2408448 | tf_op jit(solution)/shard_map/cqap,pn->cqan/dot_general | solution.py:52
  59.6 0.6 subtract_reduce_fusion.1
  60.3 3.2 %copy.67 = f32[4,2,6,1024]{2,0,1,3:T(4,128)} copy(f32[4,2,6,1024]{3,0,2,1:T(4,128)S(1)} %pad_maximum_fusion.2) | data formatting | bytes 393216 | tf_op jit(solution)/shard_map/stack | solution.py:56
  63.5 6.6 %reshape.140 = f32[64,1,768]{2,1,0:T(1,128)} reshape(f32[1024,2,4,6]{3,2,1,0:T(4,128)} %bitcast.123) | data formatting | bytes 393216
  70.1 16.5 %all-to-all-start = ((f32[64,1,768]{2,1,0:T(1,128)}), f32[64,1,768]{2,1,0:T(1,128)S(1)}, u32[]{:S(2)}, u32[]{:S(2)}) async-start(f32[64,1,768]{2,1,0:T(1,128)} %reshape.140), calls=%async_computation | async-start | bytes 393216 | tf_op jit(solution)/shard_map/all_to_all | solution.py:57
  86.6 0.0 copy-done.1
  86.6 0.1 reshape.136
  86.7 0.0 copy-done.2
  86.7 0.8 convolution_bitcast_fusion
  87.5 19.5 %all-to-all-done = f32[64,1,768]{2,1,0:T(1,128)S(1)} async-done(((f32[64,1,768]{2,1,0:T(1,128)}), f32[64,1,768]{2,1,0:T(1,128)S(1)}, u32[]{:S(2)}, u32[]{:S(2)}) %all-to-all-start) | async-done | bytes 196640 | tf_op jit(solution)/shard_map/all_to_all | solution.py:57
  107.0 0.5 broadcast.152
  107.5 1.1 reduce
  108.6 6.8 %reshape.141 = f32[1024,2,4,6]{3,2,1,0:T(4,128)} reshape(f32[64,768]{1,0:T(8,128)S(1)} %reduce) | data formatting | bytes 393216
  115.4 6.0 %copy.80 = f32[4,2,6,64,16]{4,2,1,0,3:T(8,128)} copy(f32[4,2,6,64,16]{2,0,1,4,3:T(4,128)} %bitcast.124) | data formatting | bytes 393216 | tf_op jit(solution)/shard_map/all_to_all | solution.py:57
  121.4 2.4 %reshape.134 = f32[256,192]{1,0:T(8,128)S(1)} reshape(f32[64,4,2,6,16]{4,3,2,1,0:T(8,128)} %bitcast.125) | data formatting | bytes 393216 | tf_op jit(solution)/shard_map/reshape | solution.py:60
  123.8 0.0 copy-done.3
  123.8 2.9 %fusion.5 = f32[12,256,192]{1,2,0:T(8,128)S(1)} fusion(s32[256,12]{0,1:T(8,128)S(1)} %copy-done.3, f32[256,192]{1,0:T(8,128)S(1)} %reshape.134), kind=kOutput, calls=%fused_computation.14 | convolution fusion | flops 906756096 | bytes 2568192 | tf_op jit(solution)/shard_map/ilc,cs->lis/dot_general | solution.py:66
  126.7 0.5 subtract_reduce_fusion
  127.3 1.0 copy.71
  128.3 2.1 %reshape.142 = f32[64,1,768]{2,1,0:T(1,128)S(1)} reshape(f32[256,6,2,16]{3,2,1,0:T(2,128)S(1)} %bitcast.126) | data formatting | bytes 393216
  130.4 24.6 %all_to_all.33 = f32[64,1,768]{2,1,0:T(1,128)S(1)} all-to-all(f32[64,1,768]{2,1,0:T(1,128)S(1)} %reshape.142), channel_id=1, replica_groups=mesh['clus'=64,'samp'=8] {'clus'}, dimensions={0} | all-to-all | bytes 393216 | tf_op jit(solution)/shard_map/all_to_all | solution.py:73
  155.1 1.1 reduce.1
  156.2 2.1 %reshape.143 = f32[256,6,2,16]{3,2,1,0:T(2,128)S(1)} reshape(f32[64,768]{1,0:T(8,128)S(1)} %reduce.1) | data formatting | bytes 393216
  158.3 0.1 copy.72
  158.4 0.2 copy.73
  158.6 0.8 all_to_all.30
  159.4 0.0 copy-start
  159.4 0.2 fusion.19
  159.6 0.1 copy_bitcast_fusion
  159.7 0.2 add_bitcast_fusion
  159.9 2.8 %fusion.1 = f32[32,2,6,512]{3,0,2,1:T(8,128)S(1)} fusion(f32[32,1,6,1024]{3,0,2,1:T(8,128)S(1)} %get-tuple-element.17, f32[32,1,6,1024]{3,0,2,1:T(8,128)S(1)} %get-tuple-element.16, f32[1024]{0:T(1024)S(1)} %bitcast.153, s32[1024]{0:T(1024)S(1)} %bitcast.141, f32[1024]{0:T(1024)S(1)} %bitcast.155, s32[1024]{0:T(1024)S(1)} %bitcast.143, ...), kind=kOutput, calls=%fused_computation.2 | convolution fusion | flops 1217265664 | bytes 2408448 | tf_op jit(solution)/shard_map/cqan,pn->cqap/dot_general | solution.py:77
  162.7 0.0 copy-done
  162.8 3.9 %multiply_add_fusion.3 = f32[32,2,1,512]{3,0,2,1:T(8,128)S(1)} fusion(f32[32,2,6,512]{3,0,2,1:T(8,128)S(1)} %fusion.1, f32[]{:T(128)} %bitcast.48, f32[]{:T(128)} %bitcast.39, f32[]{:T(128)} %bitcast.30, f32[]{:T(128)} %bitcast.21, f32[]{:T(128)} %bitcast.12, f32[]{:T(128)} %bitcast.3), kind=kLoop, calls=%fused_computation.39 | loop fusion | flops 360448 | bytes 917528 | tf_op jit(solution)/shard_map/add | solution.py:82
  166.7 3.9 %multiply_add_fusion.4 = f32[32,2,1,512]{3,0,2,1:T(8,128)S(1)} fusion(f32[32,2,6,512]{3,0,2,1:T(8,128)S(1)} %fusion.1, f32[]{:T(128)} %bitcast.47, f32[]{:T(128)} %bitcast.38, f32[]{:T(128)} %bitcast.29, f32[]{:T(128)} %bitcast.20, f32[]{:T(128)} %bitcast.11, f32[]{:T(128)} %bitcast.2), kind=kLoop, calls=%fused_computation.40 | loop fusion | flops 360448 | bytes 917528 | tf_op jit(solution)/shard_map/add | solution.py:82
  170.6 4.1 %multiply_add_fusion.5 = f32[32,2,1,512]{3,0,2,1:T(8,128)S(1)} fusion(f32[32,2,6,512]{3,0,2,1:T(8,128)S(1)} %fusion.1, f32[]{:T(128)} %bitcast.46, f32[]{:T(128)} %bitcast.37, f32[]{:T(128)} %bitcast.28, f32[]{:T(128)} %bitcast.19, f32[]{:T(128)} %bitcast.10, f32[]{:T(128)} %bitcast.1), kind=kLoop, calls=%fused_computation.41 | loop fusion | flops 360448 | bytes 917528 | tf_op jit(solution)/shard_map/add | solution.py:82
  174.7 3.6 %multiply_add_fusion.1 = f32[32,2,1,512]{3,0,2,1:T(8,128)S(1)} fusion(f32[32,2,6,512]{3,0,2,1:T(8,128)S(1)} %fusion.1, f32[]{:T(128)} %bitcast.53, f32[]{:T(128)} %bitcast.44, f32[]{:T(128)} %bitcast.35, f32[]{:T(128)} %bitcast.26, f32[]{:T(128)} %bitcast.17, f32[]{:T(128)} %bitcast.8), kind=kLoop, calls=%fused_computation.37 | loop fusion | flops 360448 | bytes 917528 | tf_op jit(solution)/shard_map/add | solution.py:82
  178.4 3.7 %multiply_add_fusion.2 = f32[32,2,1,512]{3,0,2,1:T(8,128)S(1)} fusion(f32[32,2,6,512]{3,0,2,1:T(8,128)S(1)} %fusion.1, f32[]{:T(128)} %bitcast.52, f32[]{:T(128)} %bitcast.43, f32[]{:T(128)} %bitcast.34, f32[]{:T(128)} %bitcast.25, f32[]{:T(128)} %bitcast.16, f32[]{:T(128)} %bitcast.7), kind=kLoop, calls=%fused_computation.38 | loop fusion | flops 360448 | bytes 917528 | tf_op jit(solution)/shard_map/add | solution.py:82
  182.1 3.8 %multiply_add_fusion = f32[32,2,1,512]{3,0,2,1:T(8,128)S(1)} fusion(f32[32,2,6,512]{3,0,2,1:T(8,128)S(1)} %fusion.1, f32[]{:T(128)} %bitcast.54, f32[]{:T(128)} %bitcast.45, f32[]{:T(128)} %bitcast.36, f32[]{:T(128)} %bitcast.27, f32[]{:T(128)} %bitcast.18, f32[]{:T(128)} %bitcast.9), kind=kLoop, calls=%fused_computation.36 | loop fusion | flops 360448 | bytes 917528 | tf_op jit(solution)/shard_map/add | solution.py:82
  185.9 3.6 %multiply_add_fusion.6 = f32[32,2,1,512]{3,0,2,1:T(8,128)S(1)} fusion(f32[32,2,6,512]{3,0,2,1:T(8,128)S(1)} %fusion.1, f32[]{:T(128)} %bitcast.51, f32[]{:T(128)} %bitcast.42, f32[]{:T(128)} %bitcast.33, f32[]{:T(128)} %bitcast.24, f32[]{:T(128)} %bitcast.15, f32[]{:T(128)} %bitcast.6), kind=kLoop, calls=%fused_computation.42 | loop fusion | flops 360448 | bytes 917528 | tf_op jit(solution)/shard_map/add | solution.py:82
  189.6 5.3 %collective-permute-start.2 = (f32[32,2,3,512]{3,0,2,1:T(8,128)S(1)}, f32[32,2,3,512]{3,0,2,1:T(8,128)S(1)}, u32[]{:S(2)}, u32[]{:S(2)}) collective-permute-start(f32[32,2,3,512]{3,0,2,1:T(8,128)S(1)} %pad_maximum_fusion), channel_id=1, source_target_pairs={{0,7},{1,0},{2,1},{3,2},{4,3},{5,4},{6,5},{7,6},{8,15},{9,8},{10,9... | collective-permute-start | bytes 1179656 | tf_op jit(solution)/shard_map/ppermute | solution.py:12
  194.9 2.8 %collective-permute-start.3 = (f32[32,2,3,512]{3,0,2,1:T(8,128)S(1)}, f32[32,2,3,512]{3,0,2,1:T(8,128)S(1)}, u32[]{:S(2)}, u32[]{:S(2)}) collective-permute-start(f32[32,2,3,512]{3,0,2,1:T(8,128)S(1)} %pad_maximum_fusion.1), channel_id=1, source_target_pairs={{0,1},{1,2},{2,3},{3,4},{4,5},{5,6},{6,7},{7,0},{8,9},{9,10},{10,1... | collective-permute-start | bytes 1179656 | tf_op jit(solution)/shard_map/ppermute | solution.py:12
  197.7 3.8 %multiply_add_fusion.7 = f32[32,2,1,512]{3,0,2,1:T(8,128)S(1)} fusion(f32[32,2,6,512]{3,0,2,1:T(8,128)S(1)} %fusion.1, f32[]{:T(128)} %bitcast.50, f32[]{:T(128)} %bitcast.41, f32[]{:T(128)} %bitcast.32, f32[]{:T(128)} %bitcast.23, f32[]{:T(128)} %bitcast.14, f32[]{:T(128)} %bitcast.5), kind=kLoop, calls=%fused_computation.43 | loop fusion | flops 360448 | bytes 917528 | tf_op jit(solution)/shard_map/add | solution.py:82
  201.5 3.9 %multiply_add_fusion.8 = f32[32,2,1,512]{3,0,2,1:T(8,128)S(1)} fusion(f32[32,2,6,512]{3,0,2,1:T(8,128)S(1)} %fusion.1, f32[]{:T(128)} %bitcast.49, f32[]{:T(128)} %bitcast.40, f32[]{:T(128)} %bitcast.31, f32[]{:T(128)} %bitcast.22, f32[]{:T(128)} %bitcast.13, f32[]{:T(128)} %bitcast.4), kind=kLoop, calls=%fused_computation.44 | loop fusion | flops 360448 | bytes 917528 | tf_op jit(solution)/shard_map/add | solution.py:82
  205.5 0.0 collective-permute-done.2
  205.5 0.0 collective-permute-done.3
  205.5 0.1 fusion.13
  205.6 1.1 copy.76
  (8 shorter events, 0.1 us)
Async XLA Ops:
  1.7 20.5 %collective-permute-start = (f32[32,2,3,512]{3,0,2,1:T(8,128)S(1)}, f32[32,2,3,512]{3,0,2,1:T(8,128)S(1)}, u32[]{:S(2)}, u32[]{:S(2)}) collective-permute-start(f32[32,2,3,512]{3,0,2,1:T(8,128)S(1)} %copy.62), channel_id=1, source_target_pairs={{0,1},{1,2},{2,3},{3,4},{4,5},{5,6},{6,7},{7,0},{8,9},{9,10},{10,1... | collective-permute-start | bytes 1179656 | tf_op jit(solution)/shard_map/ppermute | solution.py:12
  6.6 15.6 %collective-permute-start.1 = (f32[32,2,3,512]{3,0,2,1:T(8,128)S(1)}, f32[32,2,3,512]{3,0,2,1:T(8,128)S(1)}, u32[]{:S(2)}, u32[]{:S(2)}) collective-permute-start(f32[32,2,3,512]{3,0,2,1:T(8,128)S(1)} %copy.62), channel_id=1, source_target_pairs={{0,7},{1,0},{2,1},{3,2},{4,3},{5,4},{6,5},{7,6},{8,15},{9,8},{10,9... | collective-permute-start | bytes 1179656 | tf_op jit(solution)/shard_map/ppermute | solution.py:12
  63.5 23.1 %copy-start.1 = (f32[16,2,6,16]{3,1,2,0:T(2,128)S(1)}, f32[16,2,6,16]{3,1,2,0:T(2,128)}, u32[]{:S(2)}) copy-start(f32[16,2,6,16]{3,1,2,0:T(2,128)} %param.13) | copy-start | bytes 36868
  63.5 23.2 %copy-start.2 = (s32[256,12]{0,1:T(8,128)S(1)}, s32[256,12]{0,1:T(8,128)}, u32[]{:S(2)}) copy-start(s32[256,12]{0,1:T(8,128)} %param.15) | copy-start | bytes 36868
  70.1 36.9 %all-to-all-start = ((f32[64,1,768]{2,1,0:T(1,128)}), f32[64,1,768]{2,1,0:T(1,128)S(1)}, u32[]{:S(2)}, u32[]{:S(2)}) async-start(f32[64,1,768]{2,1,0:T(1,128)} %reshape.140), calls=%async_computation | async-start | bytes 393216 | tf_op jit(solution)/shard_map/all_to_all | solution.py:57
  121.4 2.4 %copy-start.3 = (s32[256,12]{0,1:T(8,128)S(1)}, s32[256,12]{0,1:T(8,128)}, u32[]{:S(2)}) copy-start(s32[256,12]{0,1:T(8,128)} %param.14) | copy-start | bytes 36868
  159.4 3.3 %copy-start = (f32[4,2,6,1024]{3,1,2,0:T(2,128)}, f32[4,2,6,1024]{3,1,2,0:T(2,128)S(1)}, u32[]{:S(2)}) copy-start(f32[4,2,6,1024]{3,1,2,0:T(2,128)S(1)} %all_to_all.30) | copy-start | bytes 589828
  189.6 15.9 %collective-permute-start.2 = (f32[32,2,3,512]{3,0,2,1:T(8,128)S(1)}, f32[32,2,3,512]{3,0,2,1:T(8,128)S(1)}, u32[]{:S(2)}, u32[]{:S(2)}) collective-permute-start(f32[32,2,3,512]{3,0,2,1:T(8,128)S(1)} %pad_maximum_fusion), channel_id=1, source_target_pairs={{0,7},{1,0},{2,1},{3,2},{4,3},{5,4},{6,5},{7,6},{8,15},{9,8},{10,9... | collective-permute-start | bytes 1179656 | tf_op jit(solution)/shard_map/ppermute | solution.py:12
  194.9 10.6 %collective-permute-start.3 = (f32[32,2,3,512]{3,0,2,1:T(8,128)S(1)}, f32[32,2,3,512]{3,0,2,1:T(8,128)S(1)}, u32[]{:S(2)}, u32[]{:S(2)}) collective-permute-start(f32[32,2,3,512]{3,0,2,1:T(8,128)S(1)} %pad_maximum_fusion.1), channel_id=1, source_target_pairs={{0,1},{1,2},{2,3},{3,4},{4,5},{5,6},{6,7},{7,0},{8,9},{9,10},{10,1... | collective-permute-start | bytes 1179656 | tf_op jit(solution)/shard_map/ppermute | solution.py:12
where the time goes:
time: 208 us; the launch traced here: 207 us
  other arithmetic  72.8 us (35%)
  local copies, waits for them, and re-layouts  44.1 us (21%)
  starting transfers between devices  35.2 us (17%)
  blocking collectives  24.6 us (12%)
  waiting for transfers between devices  19.5 us (9%)
  matrix products  9.36 us (4%)
    add x9, other arithmetic, back(): sum((theta_weights[a, b] * narrow[:, :, a] for a in range(rows_parent)))  34.5 us
    unnamed x5, other arithmetic  28.8 us
    all_to_all x1, blocking collectives, per_device(): lax.all_to_all(landed, 'clus', split_axis=0, concat_axis=3, tiled=True)  24.6 us
    unnamed x15, local copies, waits for them, and re-layouts  19.8 us
    all_to_all x1, waiting for transfers between devices, per_device(): lax.all_to_all(outgoing, 'clus', split_axis=3, concat_axis=0, tiled=True)  19.5 us
    ppermute x4, starting transfers between devices, shifted(): lax.ppermute(value, axis, [(i, (i + by) % peers) for i in range(peers)])  18.8 us
    all_to_all x1, starting transfers between devices, per_device(): lax.all_to_all(outgoing, 'clus', split_axis=3, concat_axis=0, tiled=True)  16.5 us
    all_to_all x2, local copies, waits for them, and re-layouts, per_device(): lax.all_to_all(outgoing, 'clus', split_axis=3, concat_axis=0, tiled=True)  6.5 us
  transfers between devices with their start and end apart: 5, of which 1 were waited for; matrix products, arithmetic and copies ran while one was open for 9% of the time, Pallas kernels for 0%

commit v1 on v0

--- a/solution.py
+++ b/solution.py
@@ -54,7 +54,10 @@
     real_part = refined[:, :, 0] * cosine - refined[:, :, 1] * sine
     imag_part = refined[:, :, 0] * sine + refined[:, :, 1] * cosine
     outgoing = jnp.stack([jnp.sum(real_part, axis=1), jnp.sum(imag_part, axis=1)], axis=1)
-    everyone = lax.all_to_all(outgoing, "clus", split_axis=3, concat_axis=0, tiled=True)
+    everyone = jnp.concatenate(
+        lax.all_to_all(jnp.stack(jnp.split(outgoing, lax.axis_size("clus"), axis=3)), "clus", 0, 0),
+        axis=0,
+    )
     clusters = everyone.shape[0]
     lanes = everyone.shape[2] * everyone.shape[3]
     flat = everyone.reshape(clusters, 2 * lanes)

time: 208 us -> 201 us (0.966)
  local copies, waits for them, and re-layouts: 44.1 us -> 29 us
  other arithmetic: 72.8 us -> 77.8 us
  blocking collectives: 24.6 us -> 27.8 us
  waiting for transfers between devices: 19.5 us -> 16.3 us
    unnamed x15 -> x55, local copies, waits for them, and re-layouts: 19.8 us -> 10.7 us
    unnamed x5 -> x68, other arithmetic: 28.8 us -> 33.5 us
    all_to_all x1, waiting for transfers between devices: 19.5 us -> 16.3 us  [per_device(): lax.all_to_all(jnp.stack(jnp.split(outgoing, lax.axis_size('clus'), axis=...]
    all_to_all x1, blocking collectives: 24.6 us -> 27.8 us  [per_device(): lax.all_to_all(landed, 'clus', split_axis=0, concat_axis=3, tiled=True)]
    all_to_all x2, local copies, waits for them, and re-layouts: 6.5 us -> 3.61 us  [per_device(): lax.all_to_all(jnp.stack(jnp.split(outgoing, lax.axis_size('clus'), axis=...]
    reshape x1 -> x0, local copies, waits for them, and re-layouts: 2.35 us -> none  [per_device(): flat = everyone.reshape(clusters, 2 * lanes)]
where the time goes in v1:
time: 201 us; the launch traced here: 199 us
  other arithmetic  77.8 us (39%)
  starting transfers between devices  37.2 us (19%)
  local copies, waits for them, and re-layouts  29 us (14%)
  blocking collectives  27.8 us (14%)
  waiting for transfers between devices  16.3 us (8%)
  matrix products  9.36 us (5%)
    add x9, other arithmetic, back(): sum((theta_weights[a, b] * narrow[:, :, a] for a in range(rows_parent)))  34.4 us
    unnamed x68, other arithmetic  33.5 us
    all_to_all x1, blocking collectives, per_device(): lax.all_to_all(landed, 'clus', split_axis=0, concat_axis=3, tiled=True)  27.8 us
    ppermute x4, starting transfers between devices, shifted(): lax.ppermute(value, axis, [(i, (i + by) % peers) for i in range(peers)])  20.4 us
    all_to_all x1, starting transfers between devices, per_device(): lax.all_to_all(jnp.stack(jnp.split(outgoing, lax.axis_size('clus'), axis=...  16.8 us
    all_to_all x1, waiting for transfers between devices, per_device(): lax.all_to_all(jnp.stack(jnp.split(outgoing, lax.axis_size('clus'), axis=...  16.3 us
    unnamed x55, local copies, waits for them, and re-layouts  10.7 us
    slice x3, local copies, waits for them, and re-layouts, per_device(): theta_weights[a, b] * extended[:, :, b]  6.21 us
  transfers between devices with their start and end apart: 5, of which 1 were waited for; matrix products, arithmetic and copies ran while one was open for 9% of the time, Pallas kernels for 0%

profile of v1, /device:TPU:1, one launch (start us, length us, event | category | flops | bytes accessed | tf_op | source)
XLA Modules:
  0.0 199.0 jit_solution(11224442211184242567)
XLA Ops:
  0.6 1.1 copy.252
  1.7 8.7 %collective-permute-start.1 = (f32[32,2,3,512]{3,0,2,1:T(8,128)S(1)}, f32[32,2,3,512]{3,0,2,1:T(8,128)S(1)}, u32[]{:S(2)}, u32[]{:S(2)}) collective-permute-start(f32[32,2,3,512]{3,0,2,1:T(8,128)S(1)} %copy.252), channel_id=1, source_target_pairs={{0,7},{1,0},{2,1},{3,2},{4,3},{5,4},{6,5},{7,6},{8,15},{9,8},{10,9... | collective-permute-start | bytes 1179656 | tf_op jit(solution)/shard_map/ppermute | solution.py:12
  10.5 1.9 collective-permute-start
  12.4 2.1 %fusion.88 = (f32[1,1]{1,0:T(1,128)}, f32[1,1]{1,0:T(1,128)}, f32[1,1]{1,0:T(1,128)}, f32[1,1]{1,0:T(1,128)}, f32[1,1]{1,0:T(1,128)}, /*index=5*/f32[1,1]{1,0:T(...) fusion(f32[6,9]{1,0:T(8,128)} %param.9), kind=kLoop, calls=%fused_computation.316 | loop fusion | bytes 152 | tf_op jit(solution)/shard_map/slice | solution.py:47
  14.5 1.0 fusion.85
  15.5 1.0 fusion.86
  16.6 2.0 %fusion.89 = (f32[1,1]{1,0:T(1,128)}, f32[1,1]{1,0:T(1,128)}, f32[1,1]{1,0:T(1,128)}, f32[1,1]{1,0:T(1,128)}, f32[1,1]{1,0:T(1,128)}, /*index=5*/f32[1,1]{1,0:T(...) fusion(f32[6,9]{1,0:T(8,128)} %param.9), kind=kLoop, calls=%fused_computation.317 | loop fusion | bytes 128 | tf_op jit(solution)/shard_map/slice | solution.py:47
  18.6 2.1 %fusion.87 = (f32[1,1]{1,0:T(1,128)}, f32[1,1]{1,0:T(1,128)}, f32[1,1]{1,0:T(1,128)}, f32[1,1]{1,0:T(1,128)}, f32[1,1]{1,0:T(1,128)}, /*index=5*/f32[1,1]{1,0:T(...) fusion(f32[6,9]{1,0:T(8,128)} %param.9), kind=kLoop, calls=%fused_computation.315 | loop fusion | bytes 152 | tf_op jit(solution)/shard_map/slice | solution.py:47
  20.7 1.6 fusion.84
  22.4 5.8 %constant_dynamic-update-slice_fusion.5 = f32[32,2,6,512]{3,0,2,1:T(8,128)S(1)} fusion(f32[32,2,3,512]{3,0,2,1:T(8,128)S(1)} %collective-permute-done.1, f32[32,2,3,512]{3,0,2,1:T(8,128)S(1)} %copy.252, f32[32,2,3,512]{3,0,2,1:T(8,128)S(1)} %collective-permute-done, f32[]{:T(128)} %bitcast.9, f32[]{:T(128)} %bitcast.8, f32[]{:T(128)} %bitcast.7, ...), kind=kLoop, calls=%fused_computation.166 | loop fusion | flops 557055 | bytes 1310756
  28.1 5.7 %constant_dynamic-update-slice_fusion.4 = f32[32,2,6,512]{3,0,2,1:T(8,128)S(1)} fusion(f32[32,2,6,512]{3,0,2,1:T(8,128)S(1)} %constant_dynamic-update-slice_fusion.5, f32[32,2,3,512]{3,0,2,1:T(8,128)S(1)} %collective-permute-done.1, f32[32,2,3,512]{3,0,2,1:T(8,128)S(1)} %copy.252, f32[32,2,3,512]{3,0,2,1:T(8,128)S(1)} %collective-permute-done, f32[]{:T(128)} %bitcast.18, ...), kind=kLoop, calls=%fused_computation.165 | loop fusion | flops 557056 | bytes 1310756
  33.8 5.7 %constant_dynamic-update-slice_fusion.3 = f32[32,2,6,512]{3,0,2,1:T(8,128)S(1)} fusion(f32[32,2,6,512]{3,0,2,1:T(8,128)S(1)} %constant_dynamic-update-slice_fusion.4, f32[32,2,3,512]{3,0,2,1:T(8,128)S(1)} %collective-permute-done.1, f32[32,2,3,512]{3,0,2,1:T(8,128)S(1)} %copy.252, f32[32,2,3,512]{3,0,2,1:T(8,128)S(1)} %collective-permute-done, f32[]{:T(128)} %bitcast.27, ...), kind=kLoop, calls=%fused_computation.164 | loop fusion | flops 557056 | bytes 1310756
  39.5 5.8 %constant_dynamic-update-slice_fusion.2 = f32[32,2,6,512]{3,0,2,1:T(8,128)S(1)} fusion(f32[32,2,6,512]{3,0,2,1:T(8,128)S(1)} %constant_dynamic-update-slice_fusion.3, f32[32,2,3,512]{3,0,2,1:T(8,128)S(1)} %collective-permute-done.1, f32[32,2,3,512]{3,0,2,1:T(8,128)S(1)} %copy.252, f32[32,2,3,512]{3,0,2,1:T(8,128)S(1)} %collective-permute-done, f32[]{:T(128)} %bitcast.36, ...), kind=kLoop, calls=%fused_computation.163 | loop fusion | flops 557056 | bytes 1310756
  45.3 5.6 %constant_dynamic-update-slice_fusion.1 = f32[32,2,6,512]{3,0,2,1:T(8,128)S(1)} fusion(f32[32,2,6,512]{3,0,2,1:T(8,128)S(1)} %constant_dynamic-update-slice_fusion.2, f32[32,2,3,512]{3,0,2,1:T(8,128)S(1)} %collective-permute-done.1, f32[32,2,3,512]{3,0,2,1:T(8,128)S(1)} %copy.252, f32[32,2,3,512]{3,0,2,1:T(8,128)S(1)} %collective-permute-done, f32[]{:T(128)} %bitcast.45, ...), kind=kLoop, calls=%fused_computation.162 | loop fusion | flops 557056 | bytes 1310756
  50.9 6.0 %constant_dynamic-update-slice_fusion = f32[32,2,6,512]{3,0,2,1:T(8,128)S(1)} fusion(f32[32,2,6,512]{3,0,2,1:T(8,128)S(1)} %constant_dynamic-update-slice_fusion.1, f32[32,2,3,512]{3,0,2,1:T(8,128)S(1)} %collective-permute-done.1, f32[32,2,3,512]{3,0,2,1:T(8,128)S(1)} %copy.252, f32[32,2,3,512]{3,0,2,1:T(8,128)S(1)} %collective-permute-done, f32[]{:T(128)} %bitcast.54, ...), kind=kLoop, calls=%fused_computation.161 | loop fusion | flops 557056 | bytes 1310756 | tf_op jit(solution)/shard_map/stack | solution.py:45
  57.0 2.8 %fusion.10 = f32[4,8,2,6,1024]{4,1,0,3,2:T(8,128)S(1)} fusion(f32[32,2,6,512]{3,0,2,1:T(8,128)S(1)} %constant_dynamic-update-slice_fusion, f32[1024]{0:T(1024)S(1)} %bitcast.404, s32[1024]{0:T(1024)S(1)} %bitcast.392, f32[1024]{0:T(1024)S(1)} %bitcast.406, s32[1024]{0:T(1024)S(1)} %bitcast.394, f32[1024]{0:T(1024)S(1)} %bitcast.398, ...), kind=kOutput, calls=%fused_computation.145 | convolution fusion | flops 1216872448 | bytes 2408448 | tf_op jit(solution)/shard_map/cqap,pn->cqan/dot_general | solution.py:52
  59.8 0.6 subtract_reduce_fusion.1
  60.6 0.1 constant_dynamic-update-slice_fusion.67
  60.9 0.1 constant_dynamic-update-slice_fusion.63
  61.0 0.1 constant_dynamic-update-slice_fusion.62
  61.1 0.1 constant_dynamic-update-slice_fusion.60
  61.2 0.1 constant_dynamic-update-slice_fusion.59
  61.6 0.1 constant_dynamic-update-slice_fusion.55
  61.7 0.1 constant_dynamic-update-slice_fusion.54
  61.8 0.1 constant_dynamic-update-slice_fusion.52
  62.2 0.1 constant_dynamic-update-slice_fusion.48
  62.3 0.1 constant_dynamic-update-slice_fusion.47
  65.9 1.9 reshape.135
  67.7 16.8 %all-to-all-start = ((f32[64,1,768]{2,1,0:T(1,128)}), f32[64,1,768]{2,1,0:T(1,128)S(1)}, u32[]{:S(2)}, u32[]{:S(2)}) async-start(f32[64,1,768]{2,1,0:T(1,128)} %reshape.135), calls=%async_computation | async-start | bytes 393216 | tf_op jit(solution)/shard_map/all_to_all | solution.py:58
  84.6 0.1 reshape.131
  84.7 0.8 convolution_bitcast_fusion
  85.5 16.3 %all-to-all-done = f32[64,1,768]{2,1,0:T(1,128)S(1)} async-done(((f32[64,1,768]{2,1,0:T(1,128)}), f32[64,1,768]{2,1,0:T(1,128)S(1)}, u32[]{:S(2)}, u32[]{:S(2)}) %all-to-all-start) | async-done | bytes 196640 | tf_op jit(solution)/shard_map/all_to_all | solution.py:58
  101.8 0.5 broadcast.152
  102.3 1.1 reduce
  103.4 2.2 %reshape.136 = f32[64,2,6,4,16]{4,3,2,1,0:T(4,128)} reshape(f32[64,768]{1,0:T(8,128)S(1)} %reduce) | data formatting | bytes 393216
  105.7 3.1 %copy.257 = f32[64,4,2,6,16]{4,3,2,1,0:T(8,128)} copy(f32[64,4,2,6,16]{4,1,3,2,0:T(4,128)} %bitcast.378) | data formatting | bytes 393216 | tf_op jit(solution)/shard_map/all_to_all | solution.py:58
  108.8 2.4 %reshape_reshape.3 = f32[256,192]{1,0:T(8,128)S(1)} reshape(f32[64,4,2,6,16]{4,3,2,1,0:T(8,128)} %copy.257) | data formatting | bytes 393216 | tf_op jit(solution)/shard_map/reshape;reshape | solution.py:63
  111.1 2.9 %fusion.5 = f32[12,256,192]{1,2,0:T(8,128)S(1)} fusion(s32[256,12]{0,1:T(8,128)S(1)} %copy-done.7, f32[256,192]{1,0:T(8,128)S(1)} %reshape_reshape.3), kind=kOutput, calls=%fused_computation.140 | convolution fusion | flops 906756096 | bytes 2568192 | tf_op jit(solution)/shard_map/ilc,cs->lis/dot_general | solution.py:69
  114.1 0.5 subtract_reduce_fusion
  114.6 1.0 copy.259
  115.6 2.1 %reshape.137 = f32[64,1,768]{2,1,0:T(1,128)S(1)} reshape(f32[256,6,2,16]{3,2,1,0:T(2,128)S(1)} %bitcast.379) | data formatting | bytes 393216
  117.8 27.8 %all_to_all.23 = f32[64,1,768]{2,1,0:T(1,128)S(1)} all-to-all(f32[64,1,768]{2,1,0:T(1,128)S(1)} %reshape.137), channel_id=1, replica_groups=mesh['clus'=64,'samp'=8] {'clus'}, dimensions={0} | all-to-all | bytes 393216 | tf_op jit(solution)/shard_map/all_to_all | solution.py:76
  145.5 1.1 reduce.1
  146.6 2.1 %reshape.138 = f32[256,6,2,16]{3,2,1,0:T(2,128)S(1)} reshape(f32[64,768]{1,0:T(8,128)S(1)} %reduce.1) | data formatting | bytes 393216
  148.7 0.1 copy.260
  148.9 0.2 copy.261
  149.1 0.8 all_to_all.20
  150.0 0.2 fusion.83
  150.3 0.2 add_bitcast_fusion
  150.5 0.1 copy-done.9
  150.7 2.8 %fusion.1 = f32[32,2,6,512]{3,0,2,1:T(8,128)S(1)} fusion(f32[32,1,6,1024]{3,0,2,1:T(8,128)S(1)} %get-tuple-element.17, f32[32,1,6,1024]{3,0,2,1:T(8,128)S(1)} %get-tuple-element.16, f32[1024]{0:T(1024)S(1)} %bitcast.405, s32[1024]{0:T(1024)S(1)} %bitcast.393, f32[1024]{0:T(1024)S(1)} %bitcast.407, s32[1024]{0:T(1024)S(1)} %bitcast.395, ...), kind=kOutput, calls=%fused_computation.2 | convolution fusion | flops 1217265664 | bytes 2408448 | tf_op jit(solution)/shard_map/cqan,pn->cqap/dot_general | solution.py:80
  153.6 3.8 %multiply_add_fusion.2 = f32[32,2,1,512]{3,0,2,1:T(8,128)S(1)} fusion(f32[32,2,6,512]{3,0,2,1:T(8,128)S(1)} %fusion.1, f32[]{:T(128)} %bitcast.52, f32[]{:T(128)} %bitcast.43, f32[]{:T(128)} %bitcast.34, f32[]{:T(128)} %bitcast.25, f32[]{:T(128)} %bitcast.16, f32[]{:T(128)} %bitcast.7), kind=kLoop, calls=%fused_computation.233 | loop fusion | flops 360448 | bytes 917528 | tf_op jit(solution)/shard_map/add | solution.py:85
  157.4 3.7 %multiply_add_fusion.1 = f32[32,2,1,512]{3,0,2,1:T(8,128)S(1)} fusion(f32[32,2,6,512]{3,0,2,1:T(8,128)S(1)} %fusion.1, f32[]{:T(128)} %bitcast.53, f32[]{:T(128)} %bitcast.44, f32[]{:T(128)} %bitcast.35, f32[]{:T(128)} %bitcast.26, f32[]{:T(128)} %bitcast.17, f32[]{:T(128)} %bitcast.8), kind=kLoop, calls=%fused_computation.232 | loop fusion | flops 360448 | bytes 917528 | tf_op jit(solution)/shard_map/add | solution.py:85
  161.0 3.8 %multiply_add_fusion = f32[32,2,1,512]{3,0,2,1:T(8,128)S(1)} fusion(f32[32,2,6,512]{3,0,2,1:T(8,128)S(1)} %fusion.1, f32[]{:T(128)} %bitcast.54, f32[]{:T(128)} %bitcast.45, f32[]{:T(128)} %bitcast.36, f32[]{:T(128)} %bitcast.27, f32[]{:T(128)} %bitcast.18, f32[]{:T(128)} %bitcast.9), kind=kLoop, calls=%fused_computation.231 | loop fusion | flops 360448 | bytes 917528 | tf_op jit(solution)/shard_map/add | solution.py:85
  164.9 4.0 %multiply_add_fusion.8 = f32[32,2,1,512]{3,0,2,1:T(8,128)S(1)} fusion(f32[32,2,6,512]{3,0,2,1:T(8,128)S(1)} %fusion.1, f32[]{:T(128)} %bitcast.49, f32[]{:T(128)} %bitcast.40, f32[]{:T(128)} %bitcast.31, f32[]{:T(128)} %bitcast.22, f32[]{:T(128)} %bitcast.13, f32[]{:T(128)} %bitcast.4), kind=kLoop, calls=%fused_computation.239 | loop fusion | flops 360448 | bytes 917528 | tf_op jit(solution)/shard_map/add | solution.py:85
  168.8 3.9 %multiply_add_fusion.5 = f32[32,2,1,512]{3,0,2,1:T(8,128)S(1)} fusion(f32[32,2,6,512]{3,0,2,1:T(8,128)S(1)} %fusion.1, f32[]{:T(128)} %bitcast.46, f32[]{:T(128)} %bitcast.37, f32[]{:T(128)} %bitcast.28, f32[]{:T(128)} %bitcast.19, f32[]{:T(128)} %bitcast.10, f32[]{:T(128)} %bitcast.1), kind=kLoop, calls=%fused_computation.236 | loop fusion | flops 360448 | bytes 917528 | tf_op jit(solution)/shard_map/add | solution.py:85
  172.7 3.8 %multiply_add_fusion.4 = f32[32,2,1,512]{3,0,2,1:T(8,128)S(1)} fusion(f32[32,2,6,512]{3,0,2,1:T(8,128)S(1)} %fusion.1, f32[]{:T(128)} %bitcast.47, f32[]{:T(128)} %bitcast.38, f32[]{:T(128)} %bitcast.29, f32[]{:T(128)} %bitcast.20, f32[]{:T(128)} %bitcast.11, f32[]{:T(128)} %bitcast.2), kind=kLoop, calls=%fused_computation.235 | loop fusion | flops 360448 | bytes 917528 | tf_op jit(solution)/shard_map/add | solution.py:85
  176.6 3.8 %multiply_add_fusion.3 = f32[32,2,1,512]{3,0,2,1:T(8,128)S(1)} fusion(f32[32,2,6,512]{3,0,2,1:T(8,128)S(1)} %fusion.1, f32[]{:T(128)} %bitcast.48, f32[]{:T(128)} %bitcast.39, f32[]{:T(128)} %bitcast.30, f32[]{:T(128)} %bitcast.21, f32[]{:T(128)} %bitcast.12, f32[]{:T(128)} %bitcast.3), kind=kLoop, calls=%fused_computation.234 | loop fusion | flops 360448 | bytes 917528 | tf_op jit(solution)/shard_map/add | solution.py:85
  180.4 5.4 %collective-permute-start.2 = (f32[32,2,3,512]{3,0,2,1:T(8,128)S(1)}, f32[32,2,3,512]{3,0,2,1:T(8,128)S(1)}, u32[]{:S(2)}, u32[]{:S(2)}) collective-permute-start(f32[32,2,3,512]{3,0,2,1:T(8,128)S(1)} %pad_maximum_fusion), channel_id=1, source_target_pairs={{0,7},{1,0},{2,1},{3,2},{4,3},{5,4},{6,5},{7,6},{8,15},{9,8},{10,9... | collective-permute-start | bytes 1179656 | tf_op jit(solution)/shard_map/ppermute | solution.py:12
  185.9 4.3 %collective-permute-start.3 = (f32[32,2,3,512]{3,0,2,1:T(8,128)S(1)}, f32[32,2,3,512]{3,0,2,1:T(8,128)S(1)}, u32[]{:S(2)}, u32[]{:S(2)}) collective-permute-start(f32[32,2,3,512]{3,0,2,1:T(8,128)S(1)} %pad_maximum_fusion.1), channel_id=1, source_target_pairs={{0,1},{1,2},{2,3},{3,4},{4,5},{5,6},{6,7},{7,0},{8,9},{9,10},{10,1... | collective-permute-start | bytes 1179656 | tf_op jit(solution)/shard_map/ppermute | solution.py:12
  190.2 3.9 %multiply_add_fusion.7 = f32[32,2,1,512]{3,0,2,1:T(8,128)S(1)} fusion(f32[32,2,6,512]{3,0,2,1:T(8,128)S(1)} %fusion.1, f32[]{:T(128)} %bitcast.50, f32[]{:T(128)} %bitcast.41, f32[]{:T(128)} %bitcast.32, f32[]{:T(128)} %bitcast.23, f32[]{:T(128)} %bitcast.14, f32[]{:T(128)} %bitcast.5), kind=kLoop, calls=%fused_computation.238 | loop fusion | flops 360448 | bytes 917528 | tf_op jit(solution)/shard_map/add | solution.py:85
  194.0 3.8 %multiply_add_fusion.6 = f32[32,2,1,512]{3,0,2,1:T(8,128)S(1)} fusion(f32[32,2,6,512]{3,0,2,1:T(8,128)S(1)} %fusion.1, f32[]{:T(128)} %bitcast.51, f32[]{:T(128)} %bitcast.42, f32[]{:T(128)} %bitcast.33, f32[]{:T(128)} %bitcast.24, f32[]{:T(128)} %bitcast.15, f32[]{:T(128)} %bitcast.6), kind=kLoop, calls=%fused_computation.237 | loop fusion | flops 360448 | bytes 917528 | tf_op jit(solution)/shard_map/add | solution.py:85
  197.9 0.1 fusion.13
  198.0 1.1 copy.264
  (110 shorter events, 4.6 us)
Async XLA Ops:
  1.7 20.6 %collective-permute-start.1 = (f32[32,2,3,512]{3,0,2,1:T(8,128)S(1)}, f32[32,2,3,512]{3,0,2,1:T(8,128)S(1)}, u32[]{:S(2)}, u32[]{:S(2)}) collective-permute-start(f32[32,2,3,512]{3,0,2,1:T(8,128)S(1)} %copy.252), channel_id=1, source_target_pairs={{0,7},{1,0},{2,1},{3,2},{4,3},{5,4},{6,5},{7,6},{8,15},{9,8},{10,9... | collective-permute-start | bytes 1179656 | tf_op jit(solution)/shard_map/ppermute | solution.py:12
  10.5 11.9 %collective-permute-start = (f32[32,2,3,512]{3,0,2,1:T(8,128)S(1)}, f32[32,2,3,512]{3,0,2,1:T(8,128)S(1)}, u32[]{:S(2)}, u32[]{:S(2)}) collective-permute-start(f32[32,2,3,512]{3,0,2,1:T(8,128)S(1)} %copy.252), channel_id=1, source_target_pairs={{0,1},{1,2},{2,3},{3,4},{4,5},{5,6},{6,7},{7,0},{8,9},{9,10},{10,1... | collective-permute-start | bytes 1179656 | tf_op jit(solution)/shard_map/ppermute | solution.py:12
  15.5 41.4 %copy-start.8 = (s32[1024,1]{0,1:T(1,128)}, s32[1024,1]{0,1:T(1,128)S(1)}, u32[]{:S(2)}) copy-start(s32[1024,1]{0,1:T(1,128)S(1)} %get-tuple-element.26) | copy-start | bytes 12292
  15.5 41.4 %copy-start.10 = (s32[1024,1]{0,1:T(1,128)}, s32[1024,1]{0,1:T(1,128)S(1)}, u32[]{:S(2)}) copy-start(s32[1024,1]{0,1:T(1,128)S(1)} %get-tuple-element.27) | copy-start | bytes 12292
  16.5 40.4 %copy-start.12 = (f32[1024,1]{0,1:T(1,128)}, f32[1024,1]{0,1:T(1,128)S(1)}, u32[]{:S(2)}) copy-start(f32[1024,1]{0,1:T(1,128)S(1)} %get-tuple-element.28) | copy-start | bytes 12292
  16.6 40.4 %copy-start.14 = (f32[1024,1]{0,1:T(1,128)}, f32[1024,1]{0,1:T(1,128)S(1)}, u32[]{:S(2)}) copy-start(f32[1024,1]{0,1:T(1,128)S(1)} %get-tuple-element.29) | copy-start | bytes 12292
  16.6 40.4 %copy-start.16 = (f32[1024,1]{0,1:T(1,128)}, f32[1024,1]{0,1:T(1,128)S(1)}, u32[]{:S(2)}) copy-start(f32[1024,1]{0,1:T(1,128)S(1)} %get-tuple-element.30) | copy-start | bytes 12292
  16.6 40.4 %copy-start.18 = (f32[1024,1]{0,1:T(1,128)}, f32[1024,1]{0,1:T(1,128)S(1)}, u32[]{:S(2)}) copy-start(f32[1024,1]{0,1:T(1,128)S(1)} %get-tuple-element.31) | copy-start | bytes 12292
  16.6 40.4 %copy-start.20 = (f32[1024,1]{0,1:T(1,128)}, f32[1024,1]{0,1:T(1,128)S(1)}, u32[]{:S(2)}) copy-start(f32[1024,1]{0,1:T(1,128)S(1)} %get-tuple-element.32) | copy-start | bytes 12292
  16.6 40.4 %copy-start.22 = (f32[1024,1]{0,1:T(1,128)}, f32[1024,1]{0,1:T(1,128)S(1)}, u32[]{:S(2)}) copy-start(f32[1024,1]{0,1:T(1,128)S(1)} %get-tuple-element.33) | copy-start | bytes 12292
  22.3 37.5 %copy-start = (f32[8,6,1024]{2,0,1:T(8,128)}, f32[8,6,1024]{2,0,1:T(8,128)S(1)}, u32[]{:S(2)}) copy-start(f32[8,6,1024]{2,0,1:T(8,128)S(1)} %get-tuple-element.20) | copy-start | bytes 589828
  22.3 37.5 %copy-start.2 = (f32[8,6,1024]{2,0,1:T(8,128)}, f32[8,6,1024]{2,0,1:T(8,128)S(1)}, u32[]{:S(2)}) copy-start(f32[8,6,1024]{2,0,1:T(8,128)S(1)} %get-tuple-element.21) | copy-start | bytes 589828
  65.5 19.1 %copy-start.5 = (f32[16,2,6,16]{3,1,2,0:T(2,128)S(1)}, f32[16,2,6,16]{3,1,2,0:T(2,128)}, u32[]{:S(2)}) copy-start(f32[16,2,6,16]{3,1,2,0:T(2,128)} %param.13) | copy-start | bytes 36868
  65.6 19.1 %copy-start.6 = (s32[256,12]{0,1:T(8,128)S(1)}, s32[256,12]{0,1:T(8,128)}, u32[]{:S(2)}) copy-start(s32[256,12]{0,1:T(8,128)} %param.15) | copy-start | bytes 36868
  67.7 34.1 %all-to-all-start = ((f32[64,1,768]{2,1,0:T(1,128)}), f32[64,1,768]{2,1,0:T(1,128)S(1)}, u32[]{:S(2)}, u32[]{:S(2)}) async-start(f32[64,1,768]{2,1,0:T(1,128)} %reshape.135), calls=%async_computation | async-start | bytes 393216 | tf_op jit(solution)/shard_map/all_to_all | solution.py:58
  108.8 2.4 %copy-start.7 = (s32[256,12]{0,1:T(8,128)S(1)}, s32[256,12]{0,1:T(8,128)}, u32[]{:S(2)}) copy-start(s32[256,12]{0,1:T(8,128)} %param.14) | copy-start | bytes 36868
  149.1 1.2 copy-start.1
  149.1 1.2 copy-start.3
  149.9 3.6 %copy-start.4 = (f32[4,2,6,1024]{3,1,2,0:T(2,128)}, f32[4,2,6,1024]{3,1,2,0:T(2,128)S(1)}, u32[]{:S(2)}) copy-start(f32[4,2,6,1024]{3,1,2,0:T(2,128)S(1)} %all_to_all.20) | copy-start | bytes 589828
  149.9 0.7 copy-start.9
  149.9 0.7 copy-start.11
  150.0 0.7 copy-start.13
  150.0 0.7 copy-start.15
  150.0 0.7 copy-start.17
  150.0 0.7 copy-start.19
  150.0 0.7 copy-start.21
  150.0 0.7 copy-start.23
  180.4 17.4 %collective-permute-start.2 = (f32[32,2,3,512]{3,0,2,1:T(8,128)S(1)}, f32[32,2,3,512]{3,0,2,1:T(8,128)S(1)}, u32[]{:S(2)}, u32[]{:S(2)}) collective-permute-start(f32[32,2,3,512]{3,0,2,1:T(8,128)S(1)} %pad_maximum_fusion), channel_id=1, source_target_pairs={{0,7},{1,0},{2,1},{3,2},{4,3},{5,4},{6,5},{7,6},{8,15},{9,8},{10,9... | collective-permute-start | bytes 1179656 | tf_op jit(solution)/shard_map/ppermute | solution.py:12
  185.9 12.0 %collective-permute-start.3 = (f32[32,2,3,512]{3,0,2,1:T(8,128)S(1)}, f32[32,2,3,512]{3,0,2,1:T(8,128)S(1)}, u32[]{:S(2)}, u32[]{:S(2)}) collective-permute-start(f32[32,2,3,512]{3,0,2,1:T(8,128)S(1)} %pad_maximum_fusion.1), channel_id=1, source_target_pairs={{0,1},{1,2},{2,3},{3,4},{4,5},{5,6},{6,7},{7,0},{8,9},{9,10},{10,1... | collective-permute-start | bytes 1179656 | tf_op jit(solution)/shard_map/ppermute | solution.py:12
